TPU v7x, 32 devices: a whole 2x2x4 slice. The times are simulated.
32 devices in a mesh: wrow: 16 (over z, y, x), kblk: 2 (over core).
Axes of the slice: x: 2, y: 2, z: 4, core: 2. Of those that a mesh axis runs over, the one named last changes fastest.
Arguments:
- conduction: bfloat16 [2, 4, 64, 16384], P('kblk', None, None, 'wrow'), may hold values from -6 to 6
- valence: bfloat16 [2, 4, 64, 16384], P(None, None, 'wrow', 'kblk'), may hold values from -6 to 6
- screened: bfloat16 [4, 16384, 16384], P(None, 'wrow', 'kblk'), may hold values from -0.00036621094 to 0.00036621094
- pair_block: int32 [2, 4], replicated, may hold values from 0 to 3, as said below
Outputs:
- kernel: float32 [2, 64, 256], P('kblk', 'wrow')
Inputs may be any that keep to these rules, and one draw needn't show every extreme that they name: `pair_block`: every one of the 4 blocks is selected by at least one pair and by at most 3 pairs; one block by exactly 3 pairs.
All inputs are finite; a program needn't handle non-finite values.
Results may differ from a plain program's by a relative error of at most 0.0029.
Values may be sent and summed in bfloat16 or wider, within the bound.
No kernel may reach another device: no remote copies, remote signals or barrier semaphores. Data moves between devices by JAX's collectives and lax.ppermute only.
A program may use at most 128 MiB of HBM per device.

v0:
```python
import jax
import jax.numpy as jnp
from jax import lax
from jax.sharding import PartitionSpec as P

C = 8
V = 8


def per_device(conduction, valence, screened, pair_block):
    gathered_cond = lax.all_gather(conduction, "kblk", axis=0, tiled=True)
    gathered_vale = lax.all_gather(valence, "wrow", axis=2, tiled=True)
    k_count = gathered_cond.shape[0]
    kp_count = gathered_cond.shape[1]
    pair_count = k_count * kp_count
    row_width = gathered_cond.shape[3]
    col_width = gathered_vale.shape[3]
    cond_flat = gathered_cond.reshape(pair_count, C * C, row_width)
    vale_flat = gathered_vale.reshape(pair_count, V * V, col_width)
    flat_blocks = pair_block.reshape(pair_count)
    pair_ids = jnp.arange(pair_count, dtype=jnp.int32)
    capacity = 3 * pair_count // 8
    block_count = screened.shape[0]

    def one_block(block, total):
        sort_keys = jnp.where(flat_blocks == block, 0, pair_count) + pair_ids
        chosen = jnp.argsort(sort_keys)[:capacity]
        present = (flat_blocks[chosen] == block).astype(jnp.float32)
        vale_sel = jnp.take(vale_flat, chosen, axis=0)
        cond_sel = jnp.take(cond_flat, chosen, axis=0)
        w_tile = lax.dynamic_index_in_dim(screened, block, 0, keepdims=False)
        screened_vale = jnp.einsum(
            "pvh,gh->pvg", vale_sel, w_tile, preferred_element_type=jnp.float32
        ).astype(jnp.bfloat16)
        tiles = jnp.einsum(
            "pcg,pvg->pcv", cond_sel, screened_vale, preferred_element_type=jnp.float32
        )
        placer = (pair_ids[:, None] == chosen[None, :]).astype(jnp.float32) * present[None, :]
        return total + jnp.einsum("sp,pcv->scv", placer, tiles, precision=lax.Precision.HIGHEST)

    terms = lax.fori_loop(
        0, block_count, one_block, jnp.zeros((pair_count, C * C, V * V), jnp.float32)
    )
    terms = terms.reshape(k_count, kp_count, C, C, V, V).transpose(0, 2, 4, 1, 3, 5)
    terms = terms.reshape(k_count, C * V, kp_count * C * V)
    by_block = lax.psum_scatter(terms, "kblk", scatter_dimension=0, tiled=True)
    return lax.psum_scatter(by_block, "wrow", scatter_dimension=1, tiled=True)


def solution(mesh):
    return jax.shard_map(
        per_device,
        mesh=mesh,
        in_specs=(
            P("kblk", None, None, "wrow"),
            P(None, None, "wrow", "kblk"),
            P(None, "wrow", "kblk"),
            P(),
        ),
        out_specs=P("kblk", "wrow", None),
        check_vma=False,
    )
```

profile of v0, /device:TPU:0, one launch (start us, length us, event | category | flops | bytes accessed | tf_op | source)
XLA Modules:
  0.0 346.6 jit_solution(13563379429917125649)
XLA Ops:
  6.5 0.0 all-gather.5.cloned.1.call-start
  6.5 2.2 copy.8
  8.8 0.0 all-gather.5.cloned.1.call-update
  8.8 0.0 all-gather.3.cloned.1.call-start
  8.8 0.7 all-gather.3.cloned.1.call-update
  9.5 0.0 reduce-scatter.3.cloned.1.call-start
  9.6 0.8 reshape.28
  10.4 114.8 %all-gather.5.cloned.1.call-done = bf16[2,4,64,8192]{3,1,0,2:T(4,128)(2,1)} async-done(((bf16[2,4,4,8192]{3,1,0,2:T(4,128)(2,1)}), bf16[2,4,64,8192]{3,1,0,2:T(4,128)(2,1)}) %all-gather.5.cloned.1.call-update) | async-done | bytes 8388624 | tf_op jit(solution)/shard_map/all_gather | solution.py:12
  125.2 11.2 %copy.11 = bf16[2,4,64,8192]{3,2,1,0:T(8,128)(2,1)} copy(bf16[2,4,64,8192]{3,1,0,2:T(4,128)(2,1)} %all-gather.5.cloned.1.call-done) | data formatting | bytes 16777216
  136.3 0.0 all-gather.3.cloned.1.call-done
  136.3 78.8 %while.15 = (s32[]{:T(128)}, f32[8,64,64]{2,0,1:T(8,128)S(1)}, s32[8]{0:T(128)S(1)}, bf16[8,64,1024]{2,1,0:T(8,128)(2,1)}, bf16[8,64,8192]{2,1,0:T(8,128)(2,1)},...) while((s32[]{:T(128)}, f32[8,64,64]{2,0,1:T(8,128)S(1)}, s32[8]{0:T(128)S(1)}, ...), condition=%wide.region_2.3_spmd.clone.clone, body=%wide.region_0.2_spmd.clone.clone.sunk | while | flops 3249603584 | bytes 28546016 | solution.py:41
  136.4 1.0 sort.28
  137.3 4.1 %gather_fusion = bf16[3,64,8192]{2,1,0:T(8,128)(2,1)S(1)} fusion(bf16[8,64,8192]{2,1,0:T(8,128)(2,1)} %get-tuple-element.260, s32[1024]{0:T(1024)S(1)} %pad_clamp_fusion.2), kind=kCustom, calls=%fused_computation.2.clone.clone.1 | custom fusion | bytes 6291468 | tf_op jit(solution)/shard_map/while/body/eval_jaxpr/jit(_take)/gather | solution.py:29
  141.5 10.3 %fusion.45 = bf16[3,64,1024]{2,1,0:T(8,128)(2,1)} fusion(bf16[4,1024,8192]{2,1,0:T(8,128)(2,1)} %get-tuple-element.261, s32[]{:T(128)} %get-tuple-element.248, bf16[3,64,8192]{2,1,0:T(8,128)(2,1)S(1)} %gather_fusion, pred[3]{0:T(512)(128)(4,1)S(1)} %get-tuple-element.239), kind=kOutput, calls=%fused_computation.10.clone.1 | convolution fusion | flops 3222994944 | bytes 20316676 | tf_op jit(solution)/shard_map/while/body/eval_jaxpr/pvh,gh->pvg/dot_general | solution.py:32
  151.8 1.8 gather_fusion.1
  153.6 1.3 fusion.46
  154.9 0.6 gather_fusion.2
  155.5 0.5 convolution_add_fusion.2
  156.1 1.0 sort.28
  157.1 4.1 %gather_fusion = bf16[3,64,8192]{2,1,0:T(8,128)(2,1)S(1)} fusion(bf16[8,64,8192]{2,1,0:T(8,128)(2,1)} %get-tuple-element.260, s32[1024]{0:T(1024)S(1)} %pad_clamp_fusion.2), kind=kCustom, calls=%fused_computation.2.clone.clone.1 | custom fusion | bytes 6291468 | tf_op jit(solution)/shard_map/while/body/eval_jaxpr/jit(_take)/gather | solution.py:29
  161.2 10.3 %fusion.45 = bf16[3,64,1024]{2,1,0:T(8,128)(2,1)} fusion(bf16[4,1024,8192]{2,1,0:T(8,128)(2,1)} %get-tuple-element.261, s32[]{:T(128)} %get-tuple-element.248, bf16[3,64,8192]{2,1,0:T(8,128)(2,1)S(1)} %gather_fusion, pred[3]{0:T(512)(128)(4,1)S(1)} %get-tuple-element.239), kind=kOutput, calls=%fused_computation.10.clone.1 | convolution fusion | flops 3222994944 | bytes 20316676 | tf_op jit(solution)/shard_map/while/body/eval_jaxpr/pvh,gh->pvg/dot_general | solution.py:32
  171.5 1.8 gather_fusion.1
  173.3 1.3 fusion.46
  174.6 0.6 gather_fusion.2
  175.2 0.5 convolution_add_fusion.2
  175.8 1.0 sort.28
  176.8 4.1 %gather_fusion = bf16[3,64,8192]{2,1,0:T(8,128)(2,1)S(1)} fusion(bf16[8,64,8192]{2,1,0:T(8,128)(2,1)} %get-tuple-element.260, s32[1024]{0:T(1024)S(1)} %pad_clamp_fusion.2), kind=kCustom, calls=%fused_computation.2.clone.clone.1 | custom fusion | bytes 6291468 | tf_op jit(solution)/shard_map/while/body/eval_jaxpr/jit(_take)/gather | solution.py:29
  180.9 10.3 %fusion.45 = bf16[3,64,1024]{2,1,0:T(8,128)(2,1)} fusion(bf16[4,1024,8192]{2,1,0:T(8,128)(2,1)} %get-tuple-element.261, s32[]{:T(128)} %get-tuple-element.248, bf16[3,64,8192]{2,1,0:T(8,128)(2,1)S(1)} %gather_fusion, pred[3]{0:T(512)(128)(4,1)S(1)} %get-tuple-element.239), kind=kOutput, calls=%fused_computation.10.clone.1 | convolution fusion | flops 3222994944 | bytes 20316676 | tf_op jit(solution)/shard_map/while/body/eval_jaxpr/pvh,gh->pvg/dot_general | solution.py:32
  191.2 1.8 gather_fusion.1
  193.0 1.3 fusion.46
  194.3 0.6 gather_fusion.2
  194.9 0.5 convolution_add_fusion.2
  195.5 1.0 sort.28
  196.5 4.1 %gather_fusion = bf16[3,64,8192]{2,1,0:T(8,128)(2,1)S(1)} fusion(bf16[8,64,8192]{2,1,0:T(8,128)(2,1)} %get-tuple-element.260, s32[1024]{0:T(1024)S(1)} %pad_clamp_fusion.2), kind=kCustom, calls=%fused_computation.2.clone.clone.1 | custom fusion | bytes 6291468 | tf_op jit(solution)/shard_map/while/body/eval_jaxpr/jit(_take)/gather | solution.py:29
  200.6 10.3 %fusion.45 = bf16[3,64,1024]{2,1,0:T(8,128)(2,1)} fusion(bf16[4,1024,8192]{2,1,0:T(8,128)(2,1)} %get-tuple-element.261, s32[]{:T(128)} %get-tuple-element.248, bf16[3,64,8192]{2,1,0:T(8,128)(2,1)S(1)} %gather_fusion, pred[3]{0:T(512)(128)(4,1)S(1)} %get-tuple-element.239), kind=kOutput, calls=%fused_computation.10.clone.1 | convolution fusion | flops 3222994944 | bytes 20316676 | tf_op jit(solution)/shard_map/while/body/eval_jaxpr/pvh,gh->pvg/dot_general | solution.py:32
  210.9 1.8 gather_fusion.1
  212.7 1.3 fusion.46
  214.0 0.6 gather_fusion.2
  214.7 0.5 convolution_add_fusion.2
  215.2 0.6 reshape.31
  215.8 0.0 copy-start
  215.8 3.0 copy.17
  218.8 3.5 reshape.32
  222.2 0.0 reduce-scatter.3.cloned.1.call-update
  222.2 0.0 all-reduce.3.cloned.1.call-start
  222.3 6.4 %reduce-scatter.3.cloned.1.call-done = f32[1,64,256]{2,1,0:T(8,128)} async-done(((f32[2,64,256]{2,1,0:T(8,128)}), f32[1,64,256]{2,1,0:T(8,128)}) %reduce-scatter.3.cloned.1.call-update) | async-done | bytes 65552 | tf_op jit(solution)/shard_map/reduce_scatter | solution.py:46
  228.7 0.0 all-reduce.3.cloned.1.call-update
  228.8 0.0 copy-done
  228.8 0.6 dynamic-slice
  230.0 108.7 %all-reduce.3.cloned.1.call-done = f32[1,64,256]{2,1,0:T(8,128)} async-done(((f32[1,64,256]{2,1,0:T(8,128)}), f32[1,64,256]{2,1,0:T(8,128)}) %all-reduce.3.cloned.1.call-update) | async-done | bytes 65552
  338.7 1.3 constant_dynamic-slice_fusion
  (21 shorter events, 0.1 us)
Async XLA Ops:
  6.5 118.6 %all-gather.5.cloned.1.call-start = ((), (), s32[]{:S(2)}) async-start(), calls=%async_computation.2 | async-start | bytes 8912896 | tf_op jit(solution)/shard_map/all_gather | solution.py:12
  8.8 127.6 %all-gather.3.cloned.1.call-start = ((), (), s32[]{:S(2)}) async-start(), calls=%async_computation.1 | async-start | bytes 1572864 | tf_op jit(solution)/shard_map/all_gather | solution.py:11
  9.5 219.2 %reduce-scatter.3.cloned.1.call-start = ((), (), s32[]{:S(2)}) async-start(), calls=%async_computation.3 | async-start | bytes 196608 | tf_op jit(solution)/shard_map/reduce_scatter | solution.py:46
  215.8 13.0 %copy-start = (u32[32]{0:T(128)S(1)}, u32[32]{0:T(128)}, u32[]{:S(2)}) copy-start(u32[32]{0:T(128)} %constant.81) | copy-start | bytes 388
  222.2 116.5 %all-reduce.3.cloned.1.call-start = ((), (), s32[]{:S(2)}) async-start(), calls=%async_computation.4 | async-start | bytes 131072
Sparse Core Ops, SparseCore 0:
  10.1 115.0 all-gather.4
  126.7 7.1 all-gather.2
  222.4 6.3 reduce-scatter.2
  234.1 104.6 all-reduce.2
where the time goes:
time: 347 us
  waiting for transfers between devices  231 us (67%)
  local copies, waits for them, and re-layouts  49.3 us (14%)
  matrix products  48.4 us (14%)
  between operations  13.8 us (4%)
  other arithmetic  3.96 us (1%)
    all_gather x1, waiting for transfers between devices, per_device(): gathered_vale = lax.all_gather(valence, 'wrow', axis=2, tiled=True)  115 us
    unnamed x5, waiting for transfers between devices  109 us
    dot_general x4, matrix products, one_block(): jnp.einsum('pvh,gh->pvg', vale_sel, w_tile, preferred_element_type=jnp.fl...  41.1 us
    gather x4, local copies, waits for them, and re-layouts, one_block(): vale_sel = jnp.take(vale_flat, chosen, axis=0)  16.5 us
    unnamed x6, local copies, waits for them, and re-layouts  15.3 us
    gather x4, local copies, waits for them, and re-layouts, one_block(): cond_sel = jnp.take(cond_flat, chosen, axis=0)  7.18 us
  transfers between devices with their start and end apart: 4, of which 3 were waited for; matrix products, arithmetic and copies ran while one was open for 4% of the time, Pallas kernels for 0%

commit v1 on v0

--- a/solution.py
+++ b/solution.py
@@ -9,7 +9,20 @@
 
 def per_device(conduction, valence, screened, pair_block):
     gathered_cond = lax.all_gather(conduction, "kblk", axis=0, tiled=True)
-    gathered_vale = lax.all_gather(valence, "wrow", axis=2, tiled=True)
+
+    def wall_order(on_dim, mesh_name, patch):
+        lanes = lax.axis_size(mesh_name)
+        piece_next = patch
+        store = [piece_next]
+        current_arr = sorted(((dd, (dd + 1) % lanes) for dd in range(lanes)))
+        for it in range(1, lanes):
+            piece_next = lax.ppermute(piece_next, axis_name=mesh_name, perm=current_arr)
+            store.insert(0, piece_next)
+        high = jnp.concatenate(store, on_dim)
+        outcome_arr = lax.axis_index(mesh_name) + 1
+        return jnp.roll(high, outcome_arr * patch.shape[on_dim], axis=on_dim)
+
+    gathered_vale = wall_order(2, "wrow", valence)
     k_count = gathered_cond.shape[0]
     kp_count = gathered_cond.shape[1]
     pair_count = k_count * kp_count

time: 347 us -> 541 us (1.56)
  waiting for transfers between devices: 231 us -> 340 us
  local copies, waits for them, and re-layouts: 49.3 us -> 127 us
    ppermute x0 -> x15, waiting for transfers between devices: none -> 228 us  [wall_order(): piece_next = lax.ppermute(piece_next, axis_name=mesh_name, perm=current_arr)]
    all_gather x1 -> x0, waiting for transfers between devices: 115 us -> none  [per_device(): gathered_vale = lax.all_gather(valence, 'wrow', axis=2, tiled=True)]
    concatenate x0 -> x1, local copies, waits for them, and re-layouts: none -> 76.5 us  [wall_order(): return jnp.roll(high, outcome_arr * patch.shape[on_dim], axis=on_dim)]
    dynamic_slice x0 -> x1, local copies, waits for them, and re-layouts: none -> 9.27 us  [wall_order(): return jnp.roll(high, outcome_arr * patch.shape[on_dim], axis=on_dim)]
    unnamed x6 -> x18, local copies, waits for them, and re-layouts: 15.3 us -> 7.49 us
    unnamed x5 -> x4, waiting for transfers between devices: 109 us -> 109 us
  transfers between devices with their start and end apart: 4 -> 18, of which waited for: 3 -> 17; matrix products, arithmetic and copies ran while one was open for 4% -> 16% of each run, Pallas kernels for 0% -> 0%
where the time goes in v1:
time: 541 us; the launch traced here: 536 us
  waiting for transfers between devices  340 us (63%)
  local copies, waits for them, and re-layouts  127 us (23%)
  matrix products  48.2 us (9%)
  between operations  13.9 us (3%)
    ppermute x15, waiting for transfers between devices, wall_order(): piece_next = lax.ppermute(piece_next, axis_name=mesh_name, perm=current_arr)  228 us
    unnamed x4, waiting for transfers between devices  109 us
    concatenate x1, local copies, waits for them, and re-layouts, wall_order(): return jnp.roll(high, outcome_arr * patch.shape[on_dim], axis=on_dim)  76.5 us
    dot_general x4, matrix products, one_block(): jnp.einsum('pvh,gh->pvg', vale_sel, w_tile, preferred_element_type=jnp.fl...  40.9 us
    gather x4, local copies, waits for them, and re-layouts, one_block(): vale_sel = jnp.take(vale_flat, chosen, axis=0)  16.5 us
  transfers between devices with their start and end apart: 18, of which 17 were waited for; matrix products, arithmetic and copies ran while one was open for 16% of the time, Pallas kernels for 0%

profile of v1, /device:TPU:0, one launch (start us, length us, event | category | flops | bytes accessed | tf_op | source)
XLA Modules:
  0.0 536.5 jit_solution(8452592247526096201)
XLA Ops:
  6.5 3.0 collective-permute-start
  9.5 16.1 %collective-permute-done = bf16[2,4,4,8192]{3,2,1,0:T(4,128)(2,1)S(1)} collective-permute-done((bf16[2,4,4,8192]{3,2,1,0:T(4,128)(2,1)}, bf16[2,4,4,8192]{3,2,1,0:T(4,128)(2,1)S(1)}, u32[]{:S(2)}, u32[]{:S(2)}) %collective-permute-start) | collective-permute-done | bytes 524320 | tf_op jit(solution)/shard_map/ppermute | solution.py:19
  25.6 16.7 %collective-permute-done.1 = bf16[2,4,4,8192]{3,2,1,0:T(4,128)(2,1)S(1)} collective-permute-done((bf16[2,4,4,8192]{3,2,1,0:T(4,128)(2,1)S(1)}, bf16[2,4,4,8192]{3,2,1,0:T(4,128)(2,1)S(1)}, u32[]{:S(2)}, u32[]{:S(2)}) %collective-permute-start.1) | collective-permute-done | bytes 524320 | tf_op jit(solution)/shard_map/ppermute | solution.py:19
  42.3 15.8 %collective-permute-done.2 = bf16[2,4,4,8192]{3,2,1,0:T(4,128)(2,1)S(1)} collective-permute-done((bf16[2,4,4,8192]{3,2,1,0:T(4,128)(2,1)S(1)}, bf16[2,4,4,8192]{3,2,1,0:T(4,128)(2,1)S(1)}, u32[]{:S(2)}, u32[]{:S(2)}) %collective-permute-start.2) | collective-permute-done | bytes 524320 | tf_op jit(solution)/shard_map/ppermute | solution.py:19
  58.1 15.0 %collective-permute-done.3 = bf16[2,4,4,8192]{3,2,1,0:T(4,128)(2,1)S(1)} collective-permute-done((bf16[2,4,4,8192]{3,2,1,0:T(4,128)(2,1)S(1)}, bf16[2,4,4,8192]{3,2,1,0:T(4,128)(2,1)S(1)}, u32[]{:S(2)}, u32[]{:S(2)}) %collective-permute-start.3) | collective-permute-done | bytes 524320 | tf_op jit(solution)/shard_map/ppermute | solution.py:19
  73.1 14.1 %collective-permute-done.4 = bf16[2,4,4,8192]{3,2,1,0:T(4,128)(2,1)S(1)} collective-permute-done((bf16[2,4,4,8192]{3,2,1,0:T(4,128)(2,1)S(1)}, bf16[2,4,4,8192]{3,2,1,0:T(4,128)(2,1)S(1)}, u32[]{:S(2)}, u32[]{:S(2)}) %collective-permute-start.4) | collective-permute-done | bytes 524320 | tf_op jit(solution)/shard_map/ppermute | solution.py:19
  87.2 13.3 %collective-permute-done.5 = bf16[2,4,4,8192]{3,2,1,0:T(4,128)(2,1)S(1)} collective-permute-done((bf16[2,4,4,8192]{3,2,1,0:T(4,128)(2,1)S(1)}, bf16[2,4,4,8192]{3,2,1,0:T(4,128)(2,1)S(1)}, u32[]{:S(2)}, u32[]{:S(2)}) %collective-permute-start.5) | collective-permute-done | bytes 524320 | tf_op jit(solution)/shard_map/ppermute | solution.py:19
  100.5 12.8 %collective-permute-done.6 = bf16[2,4,4,8192]{3,2,1,0:T(4,128)(2,1)S(1)} collective-permute-done((bf16[2,4,4,8192]{3,2,1,0:T(4,128)(2,1)S(1)}, bf16[2,4,4,8192]{3,2,1,0:T(4,128)(2,1)S(1)}, u32[]{:S(2)}, u32[]{:S(2)}) %collective-permute-start.6) | collective-permute-done | bytes 524320 | tf_op jit(solution)/shard_map/ppermute | solution.py:19
  113.3 0.8 copy-done
  114.1 13.1 %collective-permute-done.7 = bf16[2,4,4,8192]{3,2,1,0:T(4,128)(2,1)S(1)} collective-permute-done((bf16[2,4,4,8192]{3,2,1,0:T(4,128)(2,1)S(1)}, bf16[2,4,4,8192]{3,2,1,0:T(4,128)(2,1)S(1)}, u32[]{:S(2)}, u32[]{:S(2)}) %collective-permute-start.7) | collective-permute-done | bytes 524320 | tf_op jit(solution)/shard_map/ppermute | solution.py:19
  127.2 0.8 copy-done.1
  128.0 14.3 %collective-permute-done.8 = bf16[2,4,4,8192]{3,2,1,0:T(4,128)(2,1)S(1)} collective-permute-done((bf16[2,4,4,8192]{3,2,1,0:T(4,128)(2,1)S(1)}, bf16[2,4,4,8192]{3,2,1,0:T(4,128)(2,1)S(1)}, u32[]{:S(2)}, u32[]{:S(2)}) %collective-permute-start.8) | collective-permute-done | bytes 524320 | tf_op jit(solution)/shard_map/ppermute | solution.py:19
  142.2 0.8 copy-done.2
  143.0 15.4 %collective-permute-done.9 = bf16[2,4,4,8192]{3,2,1,0:T(4,128)(2,1)S(1)} collective-permute-done((bf16[2,4,4,8192]{3,2,1,0:T(4,128)(2,1)S(1)}, bf16[2,4,4,8192]{3,2,1,0:T(4,128)(2,1)S(1)}, u32[]{:S(2)}, u32[]{:S(2)}) %collective-permute-start.9) | collective-permute-done | bytes 524320 | tf_op jit(solution)/shard_map/ppermute | solution.py:19
  158.4 0.8 copy-done.3
  159.2 16.5 %collective-permute-done.10 = bf16[2,4,4,8192]{3,2,1,0:T(4,128)(2,1)S(1)} collective-permute-done((bf16[2,4,4,8192]{3,2,1,0:T(4,128)(2,1)S(1)}, bf16[2,4,4,8192]{3,2,1,0:T(4,128)(2,1)S(1)}, u32[]{:S(2)}, u32[]{:S(2)}) %collective-permute-start.10) | collective-permute-done | bytes 524320 | tf_op jit(solution)/shard_map/ppermute | solution.py:19
  175.8 0.8 copy-done.4
  176.6 17.7 %collective-permute-done.11 = bf16[2,4,4,8192]{3,2,1,0:T(4,128)(2,1)S(1)} collective-permute-done((bf16[2,4,4,8192]{3,2,1,0:T(4,128)(2,1)S(1)}, bf16[2,4,4,8192]{3,2,1,0:T(4,128)(2,1)S(1)}, u32[]{:S(2)}, u32[]{:S(2)}) %collective-permute-start.11) | collective-permute-done | bytes 524320 | tf_op jit(solution)/shard_map/ppermute | solution.py:19
  194.3 0.8 copy-done.5
  195.1 18.0 %collective-permute-done.12 = bf16[2,4,4,8192]{3,2,1,0:T(4,128)(2,1)S(1)} collective-permute-done((bf16[2,4,4,8192]{3,2,1,0:T(4,128)(2,1)S(1)}, bf16[2,4,4,8192]{3,2,1,0:T(4,128)(2,1)S(1)}, u32[]{:S(2)}, u32[]{:S(2)}) %collective-permute-start.12) | collective-permute-done | bytes 524320 | tf_op jit(solution)/shard_map/ppermute | solution.py:19
  213.0 0.8 copy-done.6
  213.9 16.6 %collective-permute-done.13 = bf16[2,4,4,8192]{3,2,1,0:T(4,128)(2,1)} collective-permute-done((bf16[2,4,4,8192]{3,2,1,0:T(4,128)(2,1)S(1)}, bf16[2,4,4,8192]{3,2,1,0:T(4,128)(2,1)}, u32[]{:S(2)}, u32[]{:S(2)}) %collective-permute-start.13) | collective-permute-done | bytes 524320 | tf_op jit(solution)/shard_map/ppermute | solution.py:19
  230.5 0.0 reduce-scatter.3.cloned.1.call-start
  230.6 0.8 reshape.28
  231.3 12.2 %collective-permute-done.14 = bf16[2,4,4,8192]{3,2,1,0:T(4,128)(2,1)} collective-permute-done((bf16[2,4,4,8192]{3,2,1,0:T(4,128)(2,1)}, bf16[2,4,4,8192]{3,2,1,0:T(4,128)(2,1)}, u32[]{:S(2)}, u32[]{:S(2)}) %collective-permute-start.14) | collective-permute-done | bytes 524320 | tf_op jit(solution)/shard_map/ppermute | solution.py:19
  243.6 76.5 %concatenate.6 = bf16[2,4,128,8192]{3,2,1,0:T(8,128)(2,1)} concatenate(bf16[2,4,4,8192]{3,2,1,0:T(4,128)(2,1)} %collective-permute-done.14, bf16[2,4,4,8192]{3,2,1,0:T(4,128)(2,1)} %collective-permute-done.13, bf16[2,4,4,8192]{3,2,1,0:T(4,128)(2,1)} %copy-done.6, bf16[2,4,4,8192]{3,2,1,0:T(4,128)(2,1)} %copy-done.5, bf16[2,4,4,8192]{3,2,1,0:T(4,128)(2,1)} %copy-done.4, ...), dimensions={2} | concatenate | bytes 33554432 | tf_op jit(solution)/shard_map/jit(_roll_dynamic)/concatenate | solution.py:23
  320.0 9.3 %constant_dynamic-slice_fusion.1 = bf16[2,4,64,8192]{3,2,1,0:T(8,128)(2,1)} fusion(bf16[2,4,128,8192]{3,2,1,0:T(8,128)(2,1)} %concatenate.6, s32[]{:T(128)S(6)} %select_n.56), kind=kLoop, calls=%fused_computation.35 | loop fusion | bytes 16777220 | tf_op jit(solution)/shard_map/jit(_roll_dynamic)/dynamic_slice | solution.py:23
  329.3 78.6 %while.15 = (s32[]{:T(128)}, f32[8,64,64]{2,0,1:T(8,128)S(1)}, s32[8]{0:T(128)S(1)}, bf16[8,64,1024]{2,1,0:T(8,128)(2,1)}, bf16[8,64,8192]{2,1,0:T(8,128)(2,1)},...) while((s32[]{:T(128)}, f32[8,64,64]{2,0,1:T(8,128)S(1)}, s32[8]{0:T(128)S(1)}, ...), condition=%wide.region_2.3_spmd.clone.clone, body=%wide.region_0.2_spmd.clone.clone.sunk | while | flops 3249603584 | bytes 28546016 | solution.py:54
  329.3 1.0 sort.28
  330.3 4.1 gather_fusion
  334.4 10.2 %fusion.45 = bf16[3,64,1024]{2,1,0:T(8,128)(2,1)} fusion(bf16[4,1024,8192]{2,1,0:T(8,128)(2,1)} %get-tuple-element.255, s32[]{:T(128)} %get-tuple-element.242, bf16[3,64,8192]{2,1,0:T(8,128)(2,1)S(1)} %gather_fusion, pred[3]{0:T(512)(128)(4,1)S(1)} %get-tuple-element.233), kind=kOutput, calls=%fused_computation.10.clone.1 | convolution fusion | flops 3222994944 | bytes 20316676 | tf_op jit(solution)/shard_map/while/body/eval_jaxpr/pvh,gh->pvg/dot_general | solution.py:45
  344.6 1.8 gather_fusion.1
  346.4 1.3 fusion.46
  347.7 0.6 gather_fusion.2
  348.4 0.5 convolution_add_fusion.2
  348.9 1.0 sort.28
  349.9 4.1 gather_fusion
  354.1 10.2 %fusion.45 = bf16[3,64,1024]{2,1,0:T(8,128)(2,1)} fusion(bf16[4,1024,8192]{2,1,0:T(8,128)(2,1)} %get-tuple-element.255, s32[]{:T(128)} %get-tuple-element.242, bf16[3,64,8192]{2,1,0:T(8,128)(2,1)S(1)} %gather_fusion, pred[3]{0:T(512)(128)(4,1)S(1)} %get-tuple-element.233), kind=kOutput, calls=%fused_computation.10.clone.1 | convolution fusion | flops 3222994944 | bytes 20316676 | tf_op jit(solution)/shard_map/while/body/eval_jaxpr/pvh,gh->pvg/dot_general | solution.py:45
  364.3 1.8 gather_fusion.1
  366.1 1.3 fusion.46
  367.4 0.6 gather_fusion.2
  368.0 0.5 convolution_add_fusion.2
  368.6 1.0 sort.28
  369.6 4.1 gather_fusion
  373.7 10.2 %fusion.45 = bf16[3,64,1024]{2,1,0:T(8,128)(2,1)} fusion(bf16[4,1024,8192]{2,1,0:T(8,128)(2,1)} %get-tuple-element.255, s32[]{:T(128)} %get-tuple-element.242, bf16[3,64,8192]{2,1,0:T(8,128)(2,1)S(1)} %gather_fusion, pred[3]{0:T(512)(128)(4,1)S(1)} %get-tuple-element.233), kind=kOutput, calls=%fused_computation.10.clone.1 | convolution fusion | flops 3222994944 | bytes 20316676 | tf_op jit(solution)/shard_map/while/body/eval_jaxpr/pvh,gh->pvg/dot_general | solution.py:45
  383.9 1.8 gather_fusion.1
  385.7 1.3 fusion.46
  387.1 0.6 gather_fusion.2
  387.7 0.5 convolution_add_fusion.2
  388.2 1.0 sort.28
  389.2 4.1 gather_fusion
  393.4 10.2 %fusion.45 = bf16[3,64,1024]{2,1,0:T(8,128)(2,1)} fusion(bf16[4,1024,8192]{2,1,0:T(8,128)(2,1)} %get-tuple-element.255, s32[]{:T(128)} %get-tuple-element.242, bf16[3,64,8192]{2,1,0:T(8,128)(2,1)S(1)} %gather_fusion, pred[3]{0:T(512)(128)(4,1)S(1)} %get-tuple-element.233), kind=kOutput, calls=%fused_computation.10.clone.1 | convolution fusion | flops 3222994944 | bytes 20316676 | tf_op jit(solution)/shard_map/while/body/eval_jaxpr/pvh,gh->pvg/dot_general | solution.py:45
  403.6 1.8 gather_fusion.1
  405.4 1.3 fusion.46
  406.7 0.6 gather_fusion.2
  407.4 0.5 convolution_add_fusion.2
  407.9 0.6 reshape.31
  408.5 3.0 copy.14
  411.5 3.4 reshape.32
  414.9 0.0 all-reduce.3.cloned.1.call-start
  415.0 3.6 reduce-scatter.3.cloned.1.call-done
  418.6 0.6 dynamic-slice
  419.8 108.8 %all-reduce.3.cloned.1.call-done = f32[1,64,256]{2,1,0:T(8,128)} async-done(((f32[1,64,256]{2,1,0:T(8,128)}), f32[1,64,256]{2,1,0:T(8,128)}) %all-reduce.3.cloned.1.call-update) | async-done | bytes 65552
  528.6 1.3 constant_dynamic-slice_fusion
  (49 shorter events, 0.2 us)
Async XLA Ops:
  6.5 322.7 %all-gather.2.cloned.1.call-start = ((), (), s32[]{:S(2)}) async-start(), calls=%async_computation.1 | async-start | bytes 1572864 | tf_op jit(solution)/shard_map/all_gather | solution.py:11
  6.5 19.1 %collective-permute-start = (bf16[2,4,4,8192]{3,2,1,0:T(4,128)(2,1)}, bf16[2,4,4,8192]{3,2,1,0:T(4,128)(2,1)S(1)}, u32[]{:S(2)}, u32[]{:S(2)}) collective-permute-start(bf16[2,4,4,8192]{3,2,1,0:T(4,128)(2,1)} %param.7), channel_id=1, source_target_pairs={{0,2},{2,4},{4,6},{6,8},{8,10},{10,12},{12,14},{14,16},{16,18},{18... | collective-permute-start | bytes 1572872 | tf_op jit(solution)/shard_map/ppermute | solution.py:19
  25.6 16.7 %collective-permute-start.1 = (bf16[2,4,4,8192]{3,2,1,0:T(4,128)(2,1)S(1)}, bf16[2,4,4,8192]{3,2,1,0:T(4,128)(2,1)S(1)}, u32[]{:S(2)}, u32[]{:S(2)}) collective-permute-start(bf16[2,4,4,8192]{3,2,1,0:T(4,128)(2,1)S(1)} %collective-permute-done), channel_id=1, source_target_pairs={{0,2},{2,4},{4,6},{6,8},{8,10},{10,12},{12,14},{14,16},{16,18},{18... | collective-permute-start | bytes 1572872 | tf_op jit(solution)/shard_map/ppermute | solution.py:19
  42.3 15.8 %collective-permute-start.2 = (bf16[2,4,4,8192]{3,2,1,0:T(4,128)(2,1)S(1)}, bf16[2,4,4,8192]{3,2,1,0:T(4,128)(2,1)S(1)}, u32[]{:S(2)}, u32[]{:S(2)}) collective-permute-start(bf16[2,4,4,8192]{3,2,1,0:T(4,128)(2,1)S(1)} %collective-permute-done.1), channel_id=1, source_target_pairs={{0,2},{2,4},{4,6},{6,8},{8,10},{10,12},{12,14},{14,16},{16,18},{18... | collective-permute-start | bytes 1572872 | tf_op jit(solution)/shard_map/ppermute | solution.py:19
  58.1 15.0 %collective-permute-start.3 = (bf16[2,4,4,8192]{3,2,1,0:T(4,128)(2,1)S(1)}, bf16[2,4,4,8192]{3,2,1,0:T(4,128)(2,1)S(1)}, u32[]{:S(2)}, u32[]{:S(2)}) collective-permute-start(bf16[2,4,4,8192]{3,2,1,0:T(4,128)(2,1)S(1)} %collective-permute-done.2), channel_id=1, source_target_pairs={{0,2},{2,4},{4,6},{6,8},{8,10},{10,12},{12,14},{14,16},{16,18},{18... | collective-permute-start | bytes 1572872 | tf_op jit(solution)/shard_map/ppermute | solution.py:19
  73.1 14.1 %collective-permute-start.4 = (bf16[2,4,4,8192]{3,2,1,0:T(4,128)(2,1)S(1)}, bf16[2,4,4,8192]{3,2,1,0:T(4,128)(2,1)S(1)}, u32[]{:S(2)}, u32[]{:S(2)}) collective-permute-start(bf16[2,4,4,8192]{3,2,1,0:T(4,128)(2,1)S(1)} %collective-permute-done.3), channel_id=1, source_target_pairs={{0,2},{2,4},{4,6},{6,8},{8,10},{10,12},{12,14},{14,16},{16,18},{18... | collective-permute-start | bytes 1572872 | tf_op jit(solution)/shard_map/ppermute | solution.py:19
  87.2 13.3 %collective-permute-start.5 = (bf16[2,4,4,8192]{3,2,1,0:T(4,128)(2,1)S(1)}, bf16[2,4,4,8192]{3,2,1,0:T(4,128)(2,1)S(1)}, u32[]{:S(2)}, u32[]{:S(2)}) collective-permute-start(bf16[2,4,4,8192]{3,2,1,0:T(4,128)(2,1)S(1)} %collective-permute-done.4), channel_id=1, source_target_pairs={{0,2},{2,4},{4,6},{6,8},{8,10},{10,12},{12,14},{14,16},{16,18},{18... | collective-permute-start | bytes 1572872 | tf_op jit(solution)/shard_map/ppermute | solution.py:19
  100.5 12.8 %collective-permute-start.6 = (bf16[2,4,4,8192]{3,2,1,0:T(4,128)(2,1)S(1)}, bf16[2,4,4,8192]{3,2,1,0:T(4,128)(2,1)S(1)}, u32[]{:S(2)}, u32[]{:S(2)}) collective-permute-start(bf16[2,4,4,8192]{3,2,1,0:T(4,128)(2,1)S(1)} %collective-permute-done.5), channel_id=1, source_target_pairs={{0,2},{2,4},{4,6},{6,8},{8,10},{10,12},{12,14},{14,16},{16,18},{18... | collective-permute-start | bytes 1572872 | tf_op jit(solution)/shard_map/ppermute | solution.py:19
  113.3 0.8 copy-start
  114.1 13.1 %collective-permute-start.7 = (bf16[2,4,4,8192]{3,2,1,0:T(4,128)(2,1)S(1)}, bf16[2,4,4,8192]{3,2,1,0:T(4,128)(2,1)S(1)}, u32[]{:S(2)}, u32[]{:S(2)}) collective-permute-start(bf16[2,4,4,8192]{3,2,1,0:T(4,128)(2,1)S(1)} %collective-permute-done.6), channel_id=1, source_target_pairs={{0,2},{2,4},{4,6},{6,8},{8,10},{10,12},{12,14},{14,16},{16,18},{18... | collective-permute-start | bytes 1572872 | tf_op jit(solution)/shard_map/ppermute | solution.py:19
  127.2 0.8 copy-start.1
  128.0 14.3 %collective-permute-start.8 = (bf16[2,4,4,8192]{3,2,1,0:T(4,128)(2,1)S(1)}, bf16[2,4,4,8192]{3,2,1,0:T(4,128)(2,1)S(1)}, u32[]{:S(2)}, u32[]{:S(2)}) collective-permute-start(bf16[2,4,4,8192]{3,2,1,0:T(4,128)(2,1)S(1)} %collective-permute-done.7), channel_id=1, source_target_pairs={{0,2},{2,4},{4,6},{6,8},{8,10},{10,12},{12,14},{14,16},{16,18},{18... | collective-permute-start | bytes 1572872 | tf_op jit(solution)/shard_map/ppermute | solution.py:19
  142.2 0.8 copy-start.2
  143.0 15.4 %collective-permute-start.9 = (bf16[2,4,4,8192]{3,2,1,0:T(4,128)(2,1)S(1)}, bf16[2,4,4,8192]{3,2,1,0:T(4,128)(2,1)S(1)}, u32[]{:S(2)}, u32[]{:S(2)}) collective-permute-start(bf16[2,4,4,8192]{3,2,1,0:T(4,128)(2,1)S(1)} %collective-permute-done.8), channel_id=1, source_target_pairs={{0,2},{2,4},{4,6},{6,8},{8,10},{10,12},{12,14},{14,16},{16,18},{18... | collective-permute-start | bytes 1572872 | tf_op jit(solution)/shard_map/ppermute | solution.py:19
  158.4 0.8 copy-start.3
  159.2 16.5 %collective-permute-start.10 = (bf16[2,4,4,8192]{3,2,1,0:T(4,128)(2,1)S(1)}, bf16[2,4,4,8192]{3,2,1,0:T(4,128)(2,1)S(1)}, u32[]{:S(2)}, u32[]{:S(2)}) collective-permute-start(bf16[2,4,4,8192]{3,2,1,0:T(4,128)(2,1)S(1)} %collective-permute-done.9), channel_id=1, source_target_pairs={{0,2},{2,4},{4,6},{6,8},{8,10},{10,12},{12,14},{14,16},{16,18},{18... | collective-permute-start | bytes 1572872 | tf_op jit(solution)/shard_map/ppermute | solution.py:19
  175.8 0.8 copy-start.4
  176.6 17.7 %collective-permute-start.11 = (bf16[2,4,4,8192]{3,2,1,0:T(4,128)(2,1)S(1)}, bf16[2,4,4,8192]{3,2,1,0:T(4,128)(2,1)S(1)}, u32[]{:S(2)}, u32[]{:S(2)}) collective-permute-start(bf16[2,4,4,8192]{3,2,1,0:T(4,128)(2,1)S(1)} %collective-permute-done.10), channel_id=1, source_target_pairs={{0,2},{2,4},{4,6},{6,8},{8,10},{10,12},{12,14},{14,16},{16,18},{18... | collective-permute-start | bytes 1572872 | tf_op jit(solution)/shard_map/ppermute | solution.py:19
  194.3 0.8 copy-start.5
  195.1 18.0 %collective-permute-start.12 = (bf16[2,4,4,8192]{3,2,1,0:T(4,128)(2,1)S(1)}, bf16[2,4,4,8192]{3,2,1,0:T(4,128)(2,1)S(1)}, u32[]{:S(2)}, u32[]{:S(2)}) collective-permute-start(bf16[2,4,4,8192]{3,2,1,0:T(4,128)(2,1)S(1)} %collective-permute-done.11), channel_id=1, source_target_pairs={{0,2},{2,4},{4,6},{6,8},{8,10},{10,12},{12,14},{14,16},{16,18},{18... | collective-permute-start | bytes 1572872 | tf_op jit(solution)/shard_map/ppermute | solution.py:19
  213.0 0.8 copy-start.6
  213.9 16.6 %collective-permute-start.13 = (bf16[2,4,4,8192]{3,2,1,0:T(4,128)(2,1)S(1)}, bf16[2,4,4,8192]{3,2,1,0:T(4,128)(2,1)}, u32[]{:S(2)}, u32[]{:S(2)}) collective-permute-start(bf16[2,4,4,8192]{3,2,1,0:T(4,128)(2,1)S(1)} %collective-permute-done.12), channel_id=1, source_target_pairs={{0,2},{2,4},{4,6},{6,8},{8,10},{10,12},{12,14},{14,16},{16,18},{18... | collective-permute-start | bytes 1572872 | tf_op jit(solution)/shard_map/ppermute | solution.py:19
  230.5 13.1 %collective-permute-start.14 = (bf16[2,4,4,8192]{3,2,1,0:T(4,128)(2,1)}, bf16[2,4,4,8192]{3,2,1,0:T(4,128)(2,1)}, u32[]{:S(2)}, u32[]{:S(2)}) collective-permute-start(bf16[2,4,4,8192]{3,2,1,0:T(4,128)(2,1)} %collective-permute-done.13), channel_id=1, source_target_pairs={{0,2},{2,4},{4,6},{6,8},{8,10},{10,12},{12,14},{14,16},{16,18},{18... | collective-permute-start | bytes 1572872 | tf_op jit(solution)/shard_map/ppermute | solution.py:19
  230.5 188.0 %reduce-scatter.3.cloned.1.call-start = ((), (), s32[]{:S(2)}) async-start(), calls=%async_computation.2 | async-start | bytes 196608 | tf_op jit(solution)/shard_map/reduce_scatter | solution.py:59
  408.5 10.1 %copy-start.7 = (u32[32]{0:T(128)S(1)}, u32[32]{0:T(128)}, u32[]{:S(2)}) copy-start(u32[32]{0:T(128)} %constant.112) | copy-start | bytes 388
  414.9 113.7 %all-reduce.3.cloned.1.call-start = ((), (), s32[]{:S(2)}) async-start(), calls=%async_computation.3 | async-start | bytes 131072
Sparse Core Ops, SparseCore 0:
  230.6 10.3 all-gather.1
  415.0 3.4 reduce-scatter.2
  424.0 104.5 all-reduce.2
